TPU v7x, 32 devices: a whole 2x2x4 slice. The times are simulated.
32 devices in a mesh: groups: 2 (over y), members: 4 (over z), segment: 2 (over x), rows: 2 (over core).
Axes of the slice: x: 2, y: 2, z: 4, core: 2. Of those that a mesh axis runs over, the one named last changes fastest.
Arguments:
- init_state: bfloat16 [4, 2, 77, 128], P(('groups', 'segment'), 'rows'), parts along dimension 0, may hold values from -6 to 6
- forcing_slots: bfloat16 [4, 4, 2, 2, 4, 128], P('members', ('groups', 'segment'), None, 'rows'), parts along dimension 1, may hold values from -6 to 6
- atmos_owner: int32 [4, 2], P(('groups', 'segment')), parts along dimension 0, may hold values from 0 to 3
- land_mask: int32 [4, 128], P(('groups', 'rows')), parts along dimension 0, may hold values 0 or 1
- param_index: int32 [8], P(('groups', 'members')), parts along dimension 0, may hold values from 0 to 63
- settings: float32 [64, 16], replicated, may hold values from -5 to 5
- scale_weight: float32 [16, 256], replicated, may hold values from -0.75 to 0.75
- shift_weight: float32 [16, 256], replicated, may hold values from -0.75 to 0.75
- encode_weight: bfloat16 [256, 81], replicated, may hold values from -0.625 to 0.625
- conv_weight: bfloat16 [2, 256, 2304], P('segment'), may hold values from -0.125 to 0.125
- point_weight: bfloat16 [2, 256, 256], P('segment'), may hold values from -0.375 to 0.375
- norm_gain: bfloat16 [2, 256], P('segment'), may hold values from 0.099609375 to 1.8984375
- decode_weight: bfloat16 [77, 256], replicated, may hold values from -0.1875 to 0.1875
Outputs:
- final_state: bfloat16 [4, 4, 2, 77, 128], P('members', ('groups', 'segment'), 'rows'), parts along dimension 1
- ensemble_mean: float32 [4, 2, 77, 128], P(('groups', 'segment'), 'rows'), parts along dimension 0
There are 2 independent parts, one for each index of `groups`. A program takes and returns all parts, laid end to end along the dimension named above; an argument that names none is the same for every part. Nothing has to cross between parts.
Inputs may be any that keep to these rules, and one draw needn't show every extreme that they name: `atmos_owner`: a member index of the same group. `param_index`: a row of settings.
All inputs are finite; a program needn't handle non-finite values. No bound on the sum of `land_mask` on one device may be relied on, other than what follows from the above.
Results may differ from a plain program's by a relative error of at most 0.018.
Values may be sent and summed in bfloat16 or wider, within the bound.
A program may use at most 64 MiB of HBM per device.

v0:
```python
import jax
import jax.numpy as jnp
from jax import lax
from jax.sharding import PartitionSpec as P

STEPS = 2


def padded_2(array, sides, width):
    for axis, dim in sides:
        size, length = (lax.axis_size(axis), array.shape[dim])
        up = [(i, (i + 1) % size) for i in range(size - 1)]
        down = [(j, i) for i, j in up]
        last = lax.slice_in_dim(array, length - width, length, axis=dim)
        initial = lax.slice_in_dim(array, 0, width, axis=dim)
        before = lax.ppermute(last, axis, up)
        after = lax.ppermute(initial, axis, down)
        array = jnp.concatenate([before, array, after], axis=dim)
    return array


def from_root(array, axis, root):
    mine = lax.axis_index(axis) == root
    return lax.psum(jnp.where(mine, array, jnp.zeros_like(array)), axis)


def passed_along(block, axis, distance):
    devices = range(lax.axis_size(axis))
    route = [((i - distance) % len(devices), i) for i in devices]
    return lax.ppermute(block, axis, route)


def build_taps(rimmed, spacing):
    lat_cells = rimmed.shape[0] - 2
    lon_cells = rimmed.shape[2]
    padded = jnp.pad(rimmed, ((0, 0), (0, 0), (4, 4)))
    pieces = []
    for lat_off in range(3):
        lat_band = padded[lat_off : lat_off + lat_cells]
        for lon_off in (-1, 0, 1):
            pieces.append(lax.dynamic_slice_in_dim(lat_band, 4 + lon_off * spacing, lon_cells, 2))
    return jnp.concatenate(pieces, axis=1)


def with_rim(hidden):
    return padded_2(hidden, (("rows", 0),), 1)


def local_section(rimmed, conv_here, point_here, gain_here, spacing, land_cells):
    hidden = rimmed[1:-1]
    taps = build_taps(rimmed, spacing)
    conv_out = jnp.einsum("ok,lkx->lox", conv_here, taps, preferred_element_type=jnp.float32)
    chan_mean = jnp.mean(conv_out, axis=1, keepdims=True)
    centred = conv_out - chan_mean
    spread = jnp.mean(centred * centred, axis=1, keepdims=True)
    normed = centred * lax.rsqrt(spread + 1e-05) * gain_here.astype(jnp.float32)[None, :, None]
    activated = jax.nn.gelu(normed).astype(jnp.bfloat16)
    mixed = jnp.einsum("ok,lkx->lox", point_here, activated, preferred_element_type=jnp.float32)
    return (land_cells * (hidden.astype(jnp.float32) + mixed)).astype(jnp.bfloat16)


def encode(ocean_state, forcing_now, encode_weight, cond_scale, cond_shift, land_cells):
    inputs = jnp.concatenate([ocean_state, forcing_now], axis=1)
    lifted = jnp.einsum("ok,lkx->lox", encode_weight, inputs, preferred_element_type=jnp.float32)
    return (land_cells * (lifted * cond_scale[None, :, None] + cond_shift[None, :, None])).astype(
        jnp.bfloat16
    )


def decode(ocean_state, hidden, decode_weight, land_cells):
    change = jnp.einsum("ok,lkx->lox", decode_weight, hidden, preferred_element_type=jnp.float32)
    return (ocean_state.astype(jnp.float32) + land_cells * change).astype(jnp.bfloat16)


def per_device(
    init_state,
    forcing_slots,
    atmos_owner,
    land_mask,
    param_index,
    settings,
    scale_weight,
    shift_weight,
    encode_weight,
    conv_weight,
    point_weight,
    norm_gain,
    decode_weight,
):
    land_cells = land_mask.astype(jnp.float32)[:, None, :]
    choose_row = (jnp.arange(settings.shape[0]) == param_index[0]).astype(jnp.float32)
    setting_row = jnp.dot(choose_row, settings, precision=lax.Precision.HIGHEST)
    cond_scale = 1.0 + jnp.dot(setting_row, scale_weight, precision=lax.Precision.HIGHEST)
    cond_shift = jnp.dot(setting_row, shift_weight, precision=lax.Precision.HIGHEST)
    own_slots = forcing_slots[0, 0]
    received = []
    for step_no in range(STEPS):
        received.append(from_root(own_slots[step_no], "members", atmos_owner[0, step_no]))
    forcing = jnp.stack(received, axis=0)
    ocean_state = init_state[0]
    segments = lax.axis_size("segment")
    position = lax.axis_index("segment")
    spacing = jnp.left_shift(jnp.int32(1), position % 3)
    conv_here = conv_weight[0]
    point_here = point_weight[0]
    gain_here = norm_gain[0]
    lap_ticks = segments * STEPS
    at_head = position == 0

    def tick(tick_no, carry):
        hidden, state_now, forcing_now = carry
        decoded = decode(state_now, hidden, decode_weight, land_cells)
        state_now = jnp.where(at_head & (tick_no >= segments), decoded, state_now)
        step_force = lax.dynamic_index_in_dim(
            forcing_now, jnp.minimum(tick_no // segments, STEPS - 1), 0, keepdims=False
        )
        encoded = encode(state_now, step_force, encode_weight, cond_scale, cond_shift, land_cells)
        hidden = jnp.where(at_head & (tick_no < lap_ticks), encoded, hidden)
        rimmed = with_rim(hidden)
        active = (tick_no >= position) & (tick_no - position < lap_ticks)

        def run_block():
            return local_section(rimmed, conv_here, point_here, gain_here, spacing, land_cells)

        def keep_block():
            return hidden

        hidden = lax.cond(active, run_block, keep_block)
        return passed_along((hidden, state_now, forcing_now), "segment", 1)

    start_hidden = jnp.zeros(
        (ocean_state.shape[0], conv_weight.shape[1], ocean_state.shape[2]), jnp.bfloat16
    )
    ended = lax.fori_loop(0, segments * (STEPS + 1), tick, (start_hidden, ocean_state, forcing))
    ocean_state = ended[1]
    members = lax.axis_size("members")
    ens_total = lax.psum(ocean_state.astype(jnp.float32).astype(jnp.bfloat16), "members").astype(
        jnp.float32
    )
    return (ocean_state[None, None], (ens_total / members)[None])


def solution(mesh):
    in_specs = (
        P(("groups", "segment"), "rows", None, None),
        P("members", ("groups", "segment"), None, "rows", None, None),
        P(("groups", "segment"), None),
        P(("groups", "rows"), None),
        P(("groups", "members")),
        P(),
        P(),
        P(),
        P(),
        P("segment", None, None),
        P("segment", None, None),
        P("segment", None),
        P(),
    )
    out_specs = (
        P("members", ("groups", "segment"), "rows", None, None),
        P(("groups", "segment"), "rows", None, None),
    )
    return jax.shard_map(
        per_device, mesh=mesh, in_specs=in_specs, out_specs=out_specs, check_vma=False
    )
```

profile of v0, /device:TPU:0, one launch (start us, length us, event | category | flops | bytes accessed | tf_op | source)
XLA Modules:
  0.0 127.6 jit_solution(12876457175498616522)
XLA Ops:
  1.4 1.3 %fusion.45 = (s32[1,1]{1,0:T(1,128)}, s32[1,1]{1,0:T(1,128)}) fusion(s32[1,2]{1,0:T(1,128)} %param.19), kind=kLoop, calls=%fused_computation.74 | loop fusion | bytes 16 | tf_op jit(solution)/shard_map/slice | solution.py:98
  4.7 13.5 %all-reduce.1 = (bf16[1,1,4,128]{3,2,1,0:T(4,128)(2,1)S(1)}, bf16[1,1,4,128]{3,2,1,0:T(4,128)(2,1)S(1)}) all-reduce(bf16[1,1,4,128]{3,2,1,0:T(4,128)(2,1)S(1)} %get-tuple-element.433, bf16[1,1,4,128]{3,2,1,0:T(4,128)(2,1)S(1)} %get-tuple-element.432), channel_id=1, replica_groups=mesh['groups'=2,'members'=4,'segment'=2,'rows'=2] {'members'}, use_global_device_ids=true, to_apply=%region_1.2 | all-reduce | flops 1024 | bytes 4096 | tf_op jit(solution)/shard_map/psum | solution.py:24
  22.0 88.0 %while.19 = (s32[]{:T(128)}, bf16[1,256,128]{1,2,0:T(8,128)(2,1)S(1)}, bf16[1,77,128]{2,1,0:T(8,128)(2,1)S(1)}, bf16[2,1,4,128]{3,2,1,0:T(4,128)(2,1)S(1)}, s32[...) while((s32[]{:T(128)}, ...), condition=%wide.region_7.8_spmd, body=%wide.region_2.7_spmd.sunk | while | flops 179233824 | bytes 11268149 | solution.py:134
  22.1 0.9 fusion.65
  23.0 1.0 fusion.66
  24.0 1.3 %collective-permute-start = (bf16[1,256,128]{1,2,0:T(8,128)(2,1)S(1)}, bf16[1,256,128]{1,2,0:T(8,128)(2,1)S(1)}, u32[]{:S(2)}, u32[]{:S(2)}) collective-permute-start(bf16[1,256,128]{1,2,0:T(8,128)(2,1)S(1)} %fusion.66), channel_id=1, source_target_pairs={{1,0},{3,2},{5,4},{7,6},{9,8},{11,10},{13,12},{15,14},{17,16},{19,... | collective-permute-start | bytes 196616 | tf_op jit(solution)/shard_map/while/body/eval_jaxpr/ppermute | solution.py:17
  25.3 3.0 %collective-permute-start.1 = (bf16[1,256,128]{1,2,0:T(8,128)(2,1)S(1)}, bf16[1,256,128]{1,2,0:T(8,128)(2,1)S(1)}, u32[]{:S(2)}, u32[]{:S(2)}) collective-permute-start(bf16[1,256,128]{1,2,0:T(8,128)(2,1)S(1)} %fusion.66), channel_id=1, source_target_pairs={{0,1},{2,3},{4,5},{6,7},{8,9},{10,11},{12,13},{14,15},{16,17},{18,... | collective-permute-start | bytes 196616 | tf_op jit(solution)/shard_map/while/body/eval_jaxpr/ppermute | solution.py:16
  28.4 0.9 collective-permute-done.1
  29.3 2.4 %conditional.2 = (bf16[1,256,128]{1,2,0:T(8,128)(2,1)S(1)}) conditional(s32[]{:T(128)} %convert_element_type.92, bf16[1,256,128]{1,2,0:T(8,128)(2,1)S(1)} %fusion.66, (f32[1,1,128]{2,1,0:T(1,128)S(1)}, bf16[1,256,128]{1,2,0:T(8,128)(2,1)S(1)}, bf16[3,256,128]{1,2,0:T(8,128)(2,1)S(1)}, s32[]{:T(128)}, bf16[256,2304]{1,0:T(8,128)(2,1)}, ...), branch_computations={%region_3.3_spmd, %region_4.6_spmd} | conditional | flops 168427920 | bytes 9653952 | solution.py:128
  31.8 2.0 %collective-permute-start.3 = (bf16[1,77,128]{2,1,0:T(8,128)(2,1)S(1)}, bf16[1,77,128]{2,1,0:T(8,128)(2,1)S(1)}, u32[]{:S(2)}, u32[]{:S(2)}) collective-permute-start(bf16[1,77,128]{2,1,0:T(8,128)(2,1)S(1)} %fusion.65), channel_id=1, source_target_pairs={{2,0},{0,2},{3,1},{1,3},{6,4},{4,6},{7,5},{5,7},{10,8},{8,10},{11,... | collective-permute-start | bytes 59144 | tf_op jit(solution)/shard_map/while/body/eval_jaxpr/ppermute | solution.py:30
  33.9 3.5 %collective-permute-done.4 = bf16[2,1,4,128]{3,2,1,0:T(4,128)(2,1)S(1)} collective-permute-done((bf16[2,1,4,128]{3,2,1,0:T(4,128)(2,1)S(1)}, bf16[2,1,4,128]{3,2,1,0:T(4,128)(2,1)S(1)}, u32[]{:S(2)}, u32[]{:S(2)}) %collective-permute-start.4) | collective-permute-done | bytes 2080 | tf_op jit(solution)/shard_map/while/body/eval_jaxpr/ppermute | solution.py:30
  37.4 0.9 fusion.65
  38.4 1.0 fusion.66
  39.4 1.3 %collective-permute-start = (bf16[1,256,128]{1,2,0:T(8,128)(2,1)S(1)}, bf16[1,256,128]{1,2,0:T(8,128)(2,1)S(1)}, u32[]{:S(2)}, u32[]{:S(2)}) collective-permute-start(bf16[1,256,128]{1,2,0:T(8,128)(2,1)S(1)} %fusion.66), channel_id=1, source_target_pairs={{1,0},{3,2},{5,4},{7,6},{9,8},{11,10},{13,12},{15,14},{17,16},{19,... | collective-permute-start | bytes 196616 | tf_op jit(solution)/shard_map/while/body/eval_jaxpr/ppermute | solution.py:17
  40.7 3.0 %collective-permute-start.1 = (bf16[1,256,128]{1,2,0:T(8,128)(2,1)S(1)}, bf16[1,256,128]{1,2,0:T(8,128)(2,1)S(1)}, u32[]{:S(2)}, u32[]{:S(2)}) collective-permute-start(bf16[1,256,128]{1,2,0:T(8,128)(2,1)S(1)} %fusion.66), channel_id=1, source_target_pairs={{0,1},{2,3},{4,5},{6,7},{8,9},{10,11},{12,13},{14,15},{16,17},{18,... | collective-permute-start | bytes 196616 | tf_op jit(solution)/shard_map/while/body/eval_jaxpr/ppermute | solution.py:16
  44.6 2.4 %conditional.2 = (bf16[1,256,128]{1,2,0:T(8,128)(2,1)S(1)}) conditional(s32[]{:T(128)} %convert_element_type.92, bf16[1,256,128]{1,2,0:T(8,128)(2,1)S(1)} %fusion.66, (f32[1,1,128]{2,1,0:T(1,128)S(1)}, bf16[1,256,128]{1,2,0:T(8,128)(2,1)S(1)}, bf16[3,256,128]{1,2,0:T(8,128)(2,1)S(1)}, s32[]{:T(128)}, bf16[256,2304]{1,0:T(8,128)(2,1)}, ...), branch_computations={%region_3.3_spmd, %region_4.6_spmd} | conditional | flops 168427920 | bytes 9653952 | solution.py:128
  47.3 1.8 %collective-permute-start.3 = (bf16[1,77,128]{2,1,0:T(8,128)(2,1)S(1)}, bf16[1,77,128]{2,1,0:T(8,128)(2,1)S(1)}, u32[]{:S(2)}, u32[]{:S(2)}) collective-permute-start(bf16[1,77,128]{2,1,0:T(8,128)(2,1)S(1)} %fusion.65), channel_id=1, source_target_pairs={{2,0},{0,2},{3,1},{1,3},{6,4},{4,6},{7,5},{5,7},{10,8},{8,10},{11,... | collective-permute-start | bytes 59144 | tf_op jit(solution)/shard_map/while/body/eval_jaxpr/ppermute | solution.py:30
  49.3 3.4 %collective-permute-done.4 = bf16[2,1,4,128]{3,2,1,0:T(4,128)(2,1)S(1)} collective-permute-done((bf16[2,1,4,128]{3,2,1,0:T(4,128)(2,1)S(1)}, bf16[2,1,4,128]{3,2,1,0:T(4,128)(2,1)S(1)}, u32[]{:S(2)}, u32[]{:S(2)}) %collective-permute-start.4) | collective-permute-done | bytes 2080 | tf_op jit(solution)/shard_map/while/body/eval_jaxpr/ppermute | solution.py:30
  52.7 0.9 fusion.65
  53.7 1.0 fusion.66
  54.7 1.3 %collective-permute-start = (bf16[1,256,128]{1,2,0:T(8,128)(2,1)S(1)}, bf16[1,256,128]{1,2,0:T(8,128)(2,1)S(1)}, u32[]{:S(2)}, u32[]{:S(2)}) collective-permute-start(bf16[1,256,128]{1,2,0:T(8,128)(2,1)S(1)} %fusion.66), channel_id=1, source_target_pairs={{1,0},{3,2},{5,4},{7,6},{9,8},{11,10},{13,12},{15,14},{17,16},{19,... | collective-permute-start | bytes 196616 | tf_op jit(solution)/shard_map/while/body/eval_jaxpr/ppermute | solution.py:17
  56.0 3.0 %collective-permute-start.1 = (bf16[1,256,128]{1,2,0:T(8,128)(2,1)S(1)}, bf16[1,256,128]{1,2,0:T(8,128)(2,1)S(1)}, u32[]{:S(2)}, u32[]{:S(2)}) collective-permute-start(bf16[1,256,128]{1,2,0:T(8,128)(2,1)S(1)} %fusion.66), channel_id=1, source_target_pairs={{0,1},{2,3},{4,5},{6,7},{8,9},{10,11},{12,13},{14,15},{16,17},{18,... | collective-permute-start | bytes 196616 | tf_op jit(solution)/shard_map/while/body/eval_jaxpr/ppermute | solution.py:16
  59.9 2.4 %conditional.2 = (bf16[1,256,128]{1,2,0:T(8,128)(2,1)S(1)}) conditional(s32[]{:T(128)} %convert_element_type.92, bf16[1,256,128]{1,2,0:T(8,128)(2,1)S(1)} %fusion.66, (f32[1,1,128]{2,1,0:T(1,128)S(1)}, bf16[1,256,128]{1,2,0:T(8,128)(2,1)S(1)}, bf16[3,256,128]{1,2,0:T(8,128)(2,1)S(1)}, s32[]{:T(128)}, bf16[256,2304]{1,0:T(8,128)(2,1)}, ...), branch_computations={%region_3.3_spmd, %region_4.6_spmd} | conditional | flops 168427920 | bytes 9653952 | solution.py:128
  62.6 1.8 %collective-permute-start.3 = (bf16[1,77,128]{2,1,0:T(8,128)(2,1)S(1)}, bf16[1,77,128]{2,1,0:T(8,128)(2,1)S(1)}, u32[]{:S(2)}, u32[]{:S(2)}) collective-permute-start(bf16[1,77,128]{2,1,0:T(8,128)(2,1)S(1)} %fusion.65), channel_id=1, source_target_pairs={{2,0},{0,2},{3,1},{1,3},{6,4},{4,6},{7,5},{5,7},{10,8},{8,10},{11,... | collective-permute-start | bytes 59144 | tf_op jit(solution)/shard_map/while/body/eval_jaxpr/ppermute | solution.py:30
  64.7 3.4 %collective-permute-done.4 = bf16[2,1,4,128]{3,2,1,0:T(4,128)(2,1)S(1)} collective-permute-done((bf16[2,1,4,128]{3,2,1,0:T(4,128)(2,1)S(1)}, bf16[2,1,4,128]{3,2,1,0:T(4,128)(2,1)S(1)}, u32[]{:S(2)}, u32[]{:S(2)}) %collective-permute-start.4) | collective-permute-done | bytes 2080 | tf_op jit(solution)/shard_map/while/body/eval_jaxpr/ppermute | solution.py:30
  68.1 0.9 fusion.65
  69.0 1.0 fusion.66
  70.0 1.3 %collective-permute-start = (bf16[1,256,128]{1,2,0:T(8,128)(2,1)S(1)}, bf16[1,256,128]{1,2,0:T(8,128)(2,1)S(1)}, u32[]{:S(2)}, u32[]{:S(2)}) collective-permute-start(bf16[1,256,128]{1,2,0:T(8,128)(2,1)S(1)} %fusion.66), channel_id=1, source_target_pairs={{1,0},{3,2},{5,4},{7,6},{9,8},{11,10},{13,12},{15,14},{17,16},{19,... | collective-permute-start | bytes 196616 | tf_op jit(solution)/shard_map/while/body/eval_jaxpr/ppermute | solution.py:17
  71.3 3.0 %collective-permute-start.1 = (bf16[1,256,128]{1,2,0:T(8,128)(2,1)S(1)}, bf16[1,256,128]{1,2,0:T(8,128)(2,1)S(1)}, u32[]{:S(2)}, u32[]{:S(2)}) collective-permute-start(bf16[1,256,128]{1,2,0:T(8,128)(2,1)S(1)} %fusion.66), channel_id=1, source_target_pairs={{0,1},{2,3},{4,5},{6,7},{8,9},{10,11},{12,13},{14,15},{16,17},{18,... | collective-permute-start | bytes 196616 | tf_op jit(solution)/shard_map/while/body/eval_jaxpr/ppermute | solution.py:16
  74.4 0.9 collective-permute-done.1
  75.3 2.4 %conditional.2 = (bf16[1,256,128]{1,2,0:T(8,128)(2,1)S(1)}) conditional(s32[]{:T(128)} %convert_element_type.92, bf16[1,256,128]{1,2,0:T(8,128)(2,1)S(1)} %fusion.66, (f32[1,1,128]{2,1,0:T(1,128)S(1)}, bf16[1,256,128]{1,2,0:T(8,128)(2,1)S(1)}, bf16[3,256,128]{1,2,0:T(8,128)(2,1)S(1)}, s32[]{:T(128)}, bf16[256,2304]{1,0:T(8,128)(2,1)}, ...), branch_computations={%region_3.3_spmd, %region_4.6_spmd} | conditional | flops 168427920 | bytes 9653952 | solution.py:128
  78.0 1.8 %collective-permute-start.3 = (bf16[1,77,128]{2,1,0:T(8,128)(2,1)S(1)}, bf16[1,77,128]{2,1,0:T(8,128)(2,1)S(1)}, u32[]{:S(2)}, u32[]{:S(2)}) collective-permute-start(bf16[1,77,128]{2,1,0:T(8,128)(2,1)S(1)} %fusion.65), channel_id=1, source_target_pairs={{2,0},{0,2},{3,1},{1,3},{6,4},{4,6},{7,5},{5,7},{10,8},{8,10},{11,... | collective-permute-start | bytes 59144 | tf_op jit(solution)/shard_map/while/body/eval_jaxpr/ppermute | solution.py:30
  80.0 3.4 %collective-permute-done.4 = bf16[2,1,4,128]{3,2,1,0:T(4,128)(2,1)S(1)} collective-permute-done((bf16[2,1,4,128]{3,2,1,0:T(4,128)(2,1)S(1)}, bf16[2,1,4,128]{3,2,1,0:T(4,128)(2,1)S(1)}, u32[]{:S(2)}, u32[]{:S(2)}) %collective-permute-start.4) | collective-permute-done | bytes 2080 | tf_op jit(solution)/shard_map/while/body/eval_jaxpr/ppermute | solution.py:30
  83.4 0.9 fusion.65
  84.3 1.0 fusion.66
  85.3 1.3 %collective-permute-start = (bf16[1,256,128]{1,2,0:T(8,128)(2,1)S(1)}, bf16[1,256,128]{1,2,0:T(8,128)(2,1)S(1)}, u32[]{:S(2)}, u32[]{:S(2)}) collective-permute-start(bf16[1,256,128]{1,2,0:T(8,128)(2,1)S(1)} %fusion.66), channel_id=1, source_target_pairs={{1,0},{3,2},{5,4},{7,6},{9,8},{11,10},{13,12},{15,14},{17,16},{19,... | collective-permute-start | bytes 196616 | tf_op jit(solution)/shard_map/while/body/eval_jaxpr/ppermute | solution.py:17
  86.6 3.0 %collective-permute-start.1 = (bf16[1,256,128]{1,2,0:T(8,128)(2,1)S(1)}, bf16[1,256,128]{1,2,0:T(8,128)(2,1)S(1)}, u32[]{:S(2)}, u32[]{:S(2)}) collective-permute-start(bf16[1,256,128]{1,2,0:T(8,128)(2,1)S(1)} %fusion.66), channel_id=1, source_target_pairs={{0,1},{2,3},{4,5},{6,7},{8,9},{10,11},{12,13},{14,15},{16,17},{18,... | collective-permute-start | bytes 196616 | tf_op jit(solution)/shard_map/while/body/eval_jaxpr/ppermute | solution.py:16
  90.6 2.7 %collective-permute-start.2 = (bf16[1,256,128]{1,2,0:T(8,128)(2,1)S(1)}, bf16[1,256,128]{1,2,0:T(8,128)(2,1)S(1)}, u32[]{:S(2)}, u32[]{:S(2)}) collective-permute-start(bf16[1,256,128]{1,2,0:T(8,128)(2,1)S(1)} %get-tuple-element.591), channel_id=1, source_target_pairs={{2,0},{0,2},{3,1},{1,3},{6,4},{4,6},{7,5},{5,7},{10,8},{8,10},{11,... | collective-permute-start | bytes 196616 | tf_op jit(solution)/shard_map/while/body/eval_jaxpr/ppermute | solution.py:30
  93.4 1.9 %collective-permute-start.4 = (bf16[2,1,4,128]{3,2,1,0:T(4,128)(2,1)S(1)}, bf16[2,1,4,128]{3,2,1,0:T(4,128)(2,1)S(1)}, u32[]{:S(2)}, u32[]{:S(2)}) collective-permute-start(bf16[2,1,4,128]{3,2,1,0:T(4,128)(2,1)S(1)} %copy.34), channel_id=1, source_target_pairs={{2,0},{0,2},{3,1},{1,3},{6,4},{4,6},{7,5},{5,7},{10,8},{8,10},{11,... | collective-permute-start | bytes 6152 | tf_op jit(solution)/shard_map/while/body/eval_jaxpr/ppermute | solution.py:30
  95.3 1.8 %collective-permute-done.4 = bf16[2,1,4,128]{3,2,1,0:T(4,128)(2,1)S(1)} collective-permute-done((bf16[2,1,4,128]{3,2,1,0:T(4,128)(2,1)S(1)}, bf16[2,1,4,128]{3,2,1,0:T(4,128)(2,1)S(1)}, u32[]{:S(2)}, u32[]{:S(2)}) %collective-permute-start.4) | collective-permute-done | bytes 2080 | tf_op jit(solution)/shard_map/while/body/eval_jaxpr/ppermute | solution.py:30
  97.1 0.9 fusion.65
  98.1 1.0 fusion.66
  99.1 1.3 %collective-permute-start = (bf16[1,256,128]{1,2,0:T(8,128)(2,1)S(1)}, bf16[1,256,128]{1,2,0:T(8,128)(2,1)S(1)}, u32[]{:S(2)}, u32[]{:S(2)}) collective-permute-start(bf16[1,256,128]{1,2,0:T(8,128)(2,1)S(1)} %fusion.66), channel_id=1, source_target_pairs={{1,0},{3,2},{5,4},{7,6},{9,8},{11,10},{13,12},{15,14},{17,16},{19,... | collective-permute-start | bytes 196616 | tf_op jit(solution)/shard_map/while/body/eval_jaxpr/ppermute | solution.py:17
  100.4 3.0 %collective-permute-start.1 = (bf16[1,256,128]{1,2,0:T(8,128)(2,1)S(1)}, bf16[1,256,128]{1,2,0:T(8,128)(2,1)S(1)}, u32[]{:S(2)}, u32[]{:S(2)}) collective-permute-start(bf16[1,256,128]{1,2,0:T(8,128)(2,1)S(1)} %fusion.66), channel_id=1, source_target_pairs={{0,1},{2,3},{4,5},{6,7},{8,9},{10,11},{12,13},{14,15},{16,17},{18,... | collective-permute-start | bytes 196616 | tf_op jit(solution)/shard_map/while/body/eval_jaxpr/ppermute | solution.py:16
  104.4 1.9 %collective-permute-start.2 = (bf16[1,256,128]{1,2,0:T(8,128)(2,1)S(1)}, bf16[1,256,128]{1,2,0:T(8,128)(2,1)S(1)}, u32[]{:S(2)}, u32[]{:S(2)}) collective-permute-start(bf16[1,256,128]{1,2,0:T(8,128)(2,1)S(1)} %get-tuple-element.591), channel_id=1, source_target_pairs={{2,0},{0,2},{3,1},{1,3},{6,4},{4,6},{7,5},{5,7},{10,8},{8,10},{11,... | collective-permute-start | bytes 196616 | tf_op jit(solution)/shard_map/while/body/eval_jaxpr/ppermute | solution.py:30
  106.5 1.8 %collective-permute-start.4 = (bf16[2,1,4,128]{3,2,1,0:T(4,128)(2,1)S(1)}, bf16[2,1,4,128]{3,2,1,0:T(4,128)(2,1)S(1)}, u32[]{:S(2)}, u32[]{:S(2)}) collective-permute-start(bf16[2,1,4,128]{3,2,1,0:T(4,128)(2,1)S(1)} %copy.34), channel_id=1, source_target_pairs={{2,0},{0,2},{3,1},{1,3},{6,4},{4,6},{7,5},{5,7},{10,8},{8,10},{11,... | collective-permute-start | bytes 6152 | tf_op jit(solution)/shard_map/while/body/eval_jaxpr/ppermute | solution.py:30
  108.3 1.8 %collective-permute-done.4 = bf16[2,1,4,128]{3,2,1,0:T(4,128)(2,1)S(1)} collective-permute-done((bf16[2,1,4,128]{3,2,1,0:T(4,128)(2,1)S(1)}, bf16[2,1,4,128]{3,2,1,0:T(4,128)(2,1)S(1)}, u32[]{:S(2)}, u32[]{:S(2)}) %collective-permute-start.4) | collective-permute-done | bytes 2080 | tf_op jit(solution)/shard_map/while/body/eval_jaxpr/ppermute | solution.py:30
  110.1 16.2 %psum.23 = bf16[1,77,128]{2,0,1:T(2,128)(2,1)S(1)} all-reduce(bf16[1,77,128]{2,0,1:T(2,128)(2,1)S(1)} %copy.16), channel_id=1, replica_groups=mesh['groups'=2,'members'=4,'segment'=2,'rows'=2] {'members'}, use_global_device_ids=true, to_apply=%region_8.9 | all-reduce | flops 9856 | bytes 39424 | tf_op jit(solution)/shard_map/psum | solution.py:137
  (151 shorter events, 20.7 us)
Async XLA Ops:
  0.6 19.0 %copy-start = (f32[16,256]{1,0:T(8,128)S(1)}, f32[16,256]{1,0:T(8,128)}, u32[]{:S(2)}) copy-start(f32[16,256]{1,0:T(8,128)} %param.23) | copy-start | bytes 49156
  24.0 4.4 %collective-permute-start = (bf16[1,256,128]{1,2,0:T(8,128)(2,1)S(1)}, bf16[1,256,128]{1,2,0:T(8,128)(2,1)S(1)}, u32[]{:S(2)}, u32[]{:S(2)}) collective-permute-start(bf16[1,256,128]{1,2,0:T(8,128)(2,1)S(1)} %fusion.66), channel_id=1, source_target_pairs={{1,0},{3,2},{5,4},{7,6},{9,8},{11,10},{13,12},{15,14},{17,16},{19,... | collective-permute-start | bytes 196616 | tf_op jit(solution)/shard_map/while/body/eval_jaxpr/ppermute | solution.py:17
  25.3 3.9 %collective-permute-start.1 = (bf16[1,256,128]{1,2,0:T(8,128)(2,1)S(1)}, bf16[1,256,128]{1,2,0:T(8,128)(2,1)S(1)}, u32[]{:S(2)}, u32[]{:S(2)}) collective-permute-start(bf16[1,256,128]{1,2,0:T(8,128)(2,1)S(1)} %fusion.66), channel_id=1, source_target_pairs={{0,1},{2,3},{4,5},{6,7},{8,9},{10,11},{12,13},{14,15},{16,17},{18,... | collective-permute-start | bytes 196616 | tf_op jit(solution)/shard_map/while/body/eval_jaxpr/ppermute | solution.py:16
  29.3 1.3 copy-start.1
  30.3 1.1 copy-start.2
  31.7 5.7 %collective-permute-start.2 = (bf16[1,256,128]{1,2,0:T(8,128)(2,1)S(1)}, bf16[1,256,128]{1,2,0:T(8,128)(2,1)S(1)}, u32[]{:S(2)}, u32[]{:S(2)}) collective-permute-start(bf16[1,256,128]{1,2,0:T(8,128)(2,1)S(1)} %get-tuple-element.591), channel_id=1, source_target_pairs={{2,0},{0,2},{3,1},{1,3},{6,4},{4,6},{7,5},{5,7},{10,8},{8,10},{11,... | collective-permute-start | bytes 196616 | tf_op jit(solution)/shard_map/while/body/eval_jaxpr/ppermute | solution.py:30
  31.8 5.6 %collective-permute-start.3 = (bf16[1,77,128]{2,1,0:T(8,128)(2,1)S(1)}, bf16[1,77,128]{2,1,0:T(8,128)(2,1)S(1)}, u32[]{:S(2)}, u32[]{:S(2)}) collective-permute-start(bf16[1,77,128]{2,1,0:T(8,128)(2,1)S(1)} %fusion.65), channel_id=1, source_target_pairs={{2,0},{0,2},{3,1},{1,3},{6,4},{4,6},{7,5},{5,7},{10,8},{8,10},{11,... | collective-permute-start | bytes 59144 | tf_op jit(solution)/shard_map/while/body/eval_jaxpr/ppermute | solution.py:30
  33.8 3.6 %collective-permute-start.4 = (bf16[2,1,4,128]{3,2,1,0:T(4,128)(2,1)S(1)}, bf16[2,1,4,128]{3,2,1,0:T(4,128)(2,1)S(1)}, u32[]{:S(2)}, u32[]{:S(2)}) collective-permute-start(bf16[2,1,4,128]{3,2,1,0:T(4,128)(2,1)S(1)} %copy.34), channel_id=1, source_target_pairs={{2,0},{0,2},{3,1},{1,3},{6,4},{4,6},{7,5},{5,7},{10,8},{8,10},{11,... | collective-permute-start | bytes 6152 | tf_op jit(solution)/shard_map/while/body/eval_jaxpr/ppermute | solution.py:30
  39.4 4.4 %collective-permute-start = (bf16[1,256,128]{1,2,0:T(8,128)(2,1)S(1)}, bf16[1,256,128]{1,2,0:T(8,128)(2,1)S(1)}, u32[]{:S(2)}, u32[]{:S(2)}) collective-permute-start(bf16[1,256,128]{1,2,0:T(8,128)(2,1)S(1)} %fusion.66), channel_id=1, source_target_pairs={{1,0},{3,2},{5,4},{7,6},{9,8},{11,10},{13,12},{15,14},{17,16},{19,... | collective-permute-start | bytes 196616 | tf_op jit(solution)/shard_map/while/body/eval_jaxpr/ppermute | solution.py:17
  40.7 3.9 %collective-permute-start.1 = (bf16[1,256,128]{1,2,0:T(8,128)(2,1)S(1)}, bf16[1,256,128]{1,2,0:T(8,128)(2,1)S(1)}, u32[]{:S(2)}, u32[]{:S(2)}) collective-permute-start(bf16[1,256,128]{1,2,0:T(8,128)(2,1)S(1)} %fusion.66), channel_id=1, source_target_pairs={{0,1},{2,3},{4,5},{6,7},{8,9},{10,11},{12,13},{14,15},{16,17},{18,... | collective-permute-start | bytes 196616 | tf_op jit(solution)/shard_map/while/body/eval_jaxpr/ppermute | solution.py:16
  44.6 1.3 copy-start.1
  45.6 1.1 copy-start.2
  47.0 5.7 %collective-permute-start.2 = (bf16[1,256,128]{1,2,0:T(8,128)(2,1)S(1)}, bf16[1,256,128]{1,2,0:T(8,128)(2,1)S(1)}, u32[]{:S(2)}, u32[]{:S(2)}) collective-permute-start(bf16[1,256,128]{1,2,0:T(8,128)(2,1)S(1)} %get-tuple-element.591), channel_id=1, source_target_pairs={{2,0},{0,2},{3,1},{1,3},{6,4},{4,6},{7,5},{5,7},{10,8},{8,10},{11,... | collective-permute-start | bytes 196616 | tf_op jit(solution)/shard_map/while/body/eval_jaxpr/ppermute | solution.py:30
  47.3 5.4 %collective-permute-start.3 = (bf16[1,77,128]{2,1,0:T(8,128)(2,1)S(1)}, bf16[1,77,128]{2,1,0:T(8,128)(2,1)S(1)}, u32[]{:S(2)}, u32[]{:S(2)}) collective-permute-start(bf16[1,77,128]{2,1,0:T(8,128)(2,1)S(1)} %fusion.65), channel_id=1, source_target_pairs={{2,0},{0,2},{3,1},{1,3},{6,4},{4,6},{7,5},{5,7},{10,8},{8,10},{11,... | collective-permute-start | bytes 59144 | tf_op jit(solution)/shard_map/while/body/eval_jaxpr/ppermute | solution.py:30
  49.1 3.6 %collective-permute-start.4 = (bf16[2,1,4,128]{3,2,1,0:T(4,128)(2,1)S(1)}, bf16[2,1,4,128]{3,2,1,0:T(4,128)(2,1)S(1)}, u32[]{:S(2)}, u32[]{:S(2)}) collective-permute-start(bf16[2,1,4,128]{3,2,1,0:T(4,128)(2,1)S(1)} %copy.34), channel_id=1, source_target_pairs={{2,0},{0,2},{3,1},{1,3},{6,4},{4,6},{7,5},{5,7},{10,8},{8,10},{11,... | collective-permute-start | bytes 6152 | tf_op jit(solution)/shard_map/while/body/eval_jaxpr/ppermute | solution.py:30
  54.7 4.4 %collective-permute-start = (bf16[1,256,128]{1,2,0:T(8,128)(2,1)S(1)}, bf16[1,256,128]{1,2,0:T(8,128)(2,1)S(1)}, u32[]{:S(2)}, u32[]{:S(2)}) collective-permute-start(bf16[1,256,128]{1,2,0:T(8,128)(2,1)S(1)} %fusion.66), channel_id=1, source_target_pairs={{1,0},{3,2},{5,4},{7,6},{9,8},{11,10},{13,12},{15,14},{17,16},{19,... | collective-permute-start | bytes 196616 | tf_op jit(solution)/shard_map/while/body/eval_jaxpr/ppermute | solution.py:17
  56.0 3.9 %collective-permute-start.1 = (bf16[1,256,128]{1,2,0:T(8,128)(2,1)S(1)}, bf16[1,256,128]{1,2,0:T(8,128)(2,1)S(1)}, u32[]{:S(2)}, u32[]{:S(2)}) collective-permute-start(bf16[1,256,128]{1,2,0:T(8,128)(2,1)S(1)} %fusion.66), channel_id=1, source_target_pairs={{0,1},{2,3},{4,5},{6,7},{8,9},{10,11},{12,13},{14,15},{16,17},{18,... | collective-permute-start | bytes 196616 | tf_op jit(solution)/shard_map/while/body/eval_jaxpr/ppermute | solution.py:16
  60.0 1.3 copy-start.1
  61.0 1.1 copy-start.2
  62.4 5.7 %collective-permute-start.2 = (bf16[1,256,128]{1,2,0:T(8,128)(2,1)S(1)}, bf16[1,256,128]{1,2,0:T(8,128)(2,1)S(1)}, u32[]{:S(2)}, u32[]{:S(2)}) collective-permute-start(bf16[1,256,128]{1,2,0:T(8,128)(2,1)S(1)} %get-tuple-element.591), channel_id=1, source_target_pairs={{2,0},{0,2},{3,1},{1,3},{6,4},{4,6},{7,5},{5,7},{10,8},{8,10},{11,... | collective-permute-start | bytes 196616 | tf_op jit(solution)/shard_map/while/body/eval_jaxpr/ppermute | solution.py:30
  62.6 5.4 %collective-permute-start.3 = (bf16[1,77,128]{2,1,0:T(8,128)(2,1)S(1)}, bf16[1,77,128]{2,1,0:T(8,128)(2,1)S(1)}, u32[]{:S(2)}, u32[]{:S(2)}) collective-permute-start(bf16[1,77,128]{2,1,0:T(8,128)(2,1)S(1)} %fusion.65), channel_id=1, source_target_pairs={{2,0},{0,2},{3,1},{1,3},{6,4},{4,6},{7,5},{5,7},{10,8},{8,10},{11,... | collective-permute-start | bytes 59144 | tf_op jit(solution)/shard_map/while/body/eval_jaxpr/ppermute | solution.py:30
  64.4 3.6 %collective-permute-start.4 = (bf16[2,1,4,128]{3,2,1,0:T(4,128)(2,1)S(1)}, bf16[2,1,4,128]{3,2,1,0:T(4,128)(2,1)S(1)}, u32[]{:S(2)}, u32[]{:S(2)}) collective-permute-start(bf16[2,1,4,128]{3,2,1,0:T(4,128)(2,1)S(1)} %copy.34), channel_id=1, source_target_pairs={{2,0},{0,2},{3,1},{1,3},{6,4},{4,6},{7,5},{5,7},{10,8},{8,10},{11,... | collective-permute-start | bytes 6152 | tf_op jit(solution)/shard_map/while/body/eval_jaxpr/ppermute | solution.py:30
  70.0 4.4 %collective-permute-start = (bf16[1,256,128]{1,2,0:T(8,128)(2,1)S(1)}, bf16[1,256,128]{1,2,0:T(8,128)(2,1)S(1)}, u32[]{:S(2)}, u32[]{:S(2)}) collective-permute-start(bf16[1,256,128]{1,2,0:T(8,128)(2,1)S(1)} %fusion.66), channel_id=1, source_target_pairs={{1,0},{3,2},{5,4},{7,6},{9,8},{11,10},{13,12},{15,14},{17,16},{19,... | collective-permute-start | bytes 196616 | tf_op jit(solution)/shard_map/while/body/eval_jaxpr/ppermute | solution.py:17
  71.3 3.9 %collective-permute-start.1 = (bf16[1,256,128]{1,2,0:T(8,128)(2,1)S(1)}, bf16[1,256,128]{1,2,0:T(8,128)(2,1)S(1)}, u32[]{:S(2)}, u32[]{:S(2)}) collective-permute-start(bf16[1,256,128]{1,2,0:T(8,128)(2,1)S(1)} %fusion.66), channel_id=1, source_target_pairs={{0,1},{2,3},{4,5},{6,7},{8,9},{10,11},{12,13},{14,15},{16,17},{18,... | collective-permute-start | bytes 196616 | tf_op jit(solution)/shard_map/while/body/eval_jaxpr/ppermute | solution.py:16
  75.3 1.3 copy-start.1
  76.3 1.1 copy-start.2
  77.7 5.7 %collective-permute-start.2 = (bf16[1,256,128]{1,2,0:T(8,128)(2,1)S(1)}, bf16[1,256,128]{1,2,0:T(8,128)(2,1)S(1)}, u32[]{:S(2)}, u32[]{:S(2)}) collective-permute-start(bf16[1,256,128]{1,2,0:T(8,128)(2,1)S(1)} %get-tuple-element.591), channel_id=1, source_target_pairs={{2,0},{0,2},{3,1},{1,3},{6,4},{4,6},{7,5},{5,7},{10,8},{8,10},{11,... | collective-permute-start | bytes 196616 | tf_op jit(solution)/shard_map/while/body/eval_jaxpr/ppermute | solution.py:30
  78.0 5.4 %collective-permute-start.3 = (bf16[1,77,128]{2,1,0:T(8,128)(2,1)S(1)}, bf16[1,77,128]{2,1,0:T(8,128)(2,1)S(1)}, u32[]{:S(2)}, u32[]{:S(2)}) collective-permute-start(bf16[1,77,128]{2,1,0:T(8,128)(2,1)S(1)} %fusion.65), channel_id=1, source_target_pairs={{2,0},{0,2},{3,1},{1,3},{6,4},{4,6},{7,5},{5,7},{10,8},{8,10},{11,... | collective-permute-start | bytes 59144 | tf_op jit(solution)/shard_map/while/body/eval_jaxpr/ppermute | solution.py:30
  79.8 3.6 %collective-permute-start.4 = (bf16[2,1,4,128]{3,2,1,0:T(4,128)(2,1)S(1)}, bf16[2,1,4,128]{3,2,1,0:T(4,128)(2,1)S(1)}, u32[]{:S(2)}, u32[]{:S(2)}) collective-permute-start(bf16[2,1,4,128]{3,2,1,0:T(4,128)(2,1)S(1)} %copy.34), channel_id=1, source_target_pairs={{2,0},{0,2},{3,1},{1,3},{6,4},{4,6},{7,5},{5,7},{10,8},{8,10},{11,... | collective-permute-start | bytes 6152 | tf_op jit(solution)/shard_map/while/body/eval_jaxpr/ppermute | solution.py:30
  85.3 4.4 %collective-permute-start = (bf16[1,256,128]{1,2,0:T(8,128)(2,1)S(1)}, bf16[1,256,128]{1,2,0:T(8,128)(2,1)S(1)}, u32[]{:S(2)}, u32[]{:S(2)}) collective-permute-start(bf16[1,256,128]{1,2,0:T(8,128)(2,1)S(1)} %fusion.66), channel_id=1, source_target_pairs={{1,0},{3,2},{5,4},{7,6},{9,8},{11,10},{13,12},{15,14},{17,16},{19,... | collective-permute-start | bytes 196616 | tf_op jit(solution)/shard_map/while/body/eval_jaxpr/ppermute | solution.py:17
  86.6 3.9 %collective-permute-start.1 = (bf16[1,256,128]{1,2,0:T(8,128)(2,1)S(1)}, bf16[1,256,128]{1,2,0:T(8,128)(2,1)S(1)}, u32[]{:S(2)}, u32[]{:S(2)}) collective-permute-start(bf16[1,256,128]{1,2,0:T(8,128)(2,1)S(1)} %fusion.66), channel_id=1, source_target_pairs={{0,1},{2,3},{4,5},{6,7},{8,9},{10,11},{12,13},{14,15},{16,17},{18,... | collective-permute-start | bytes 196616 | tf_op jit(solution)/shard_map/while/body/eval_jaxpr/ppermute | solution.py:16
  90.6 6.5 %collective-permute-start.2 = (bf16[1,256,128]{1,2,0:T(8,128)(2,1)S(1)}, bf16[1,256,128]{1,2,0:T(8,128)(2,1)S(1)}, u32[]{:S(2)}, u32[]{:S(2)}) collective-permute-start(bf16[1,256,128]{1,2,0:T(8,128)(2,1)S(1)} %get-tuple-element.591), channel_id=1, source_target_pairs={{2,0},{0,2},{3,1},{1,3},{6,4},{4,6},{7,5},{5,7},{10,8},{8,10},{11,... | collective-permute-start | bytes 196616 | tf_op jit(solution)/shard_map/while/body/eval_jaxpr/ppermute | solution.py:30
  93.3 3.8 %collective-permute-start.3 = (bf16[1,77,128]{2,1,0:T(8,128)(2,1)S(1)}, bf16[1,77,128]{2,1,0:T(8,128)(2,1)S(1)}, u32[]{:S(2)}, u32[]{:S(2)}) collective-permute-start(bf16[1,77,128]{2,1,0:T(8,128)(2,1)S(1)} %fusion.65), channel_id=1, source_target_pairs={{2,0},{0,2},{3,1},{1,3},{6,4},{4,6},{7,5},{5,7},{10,8},{8,10},{11,... | collective-permute-start | bytes 59144 | tf_op jit(solution)/shard_map/while/body/eval_jaxpr/ppermute | solution.py:30
  93.4 3.7 %collective-permute-start.4 = (bf16[2,1,4,128]{3,2,1,0:T(4,128)(2,1)S(1)}, bf16[2,1,4,128]{3,2,1,0:T(4,128)(2,1)S(1)}, u32[]{:S(2)}, u32[]{:S(2)}) collective-permute-start(bf16[2,1,4,128]{3,2,1,0:T(4,128)(2,1)S(1)} %copy.34), channel_id=1, source_target_pairs={{2,0},{0,2},{3,1},{1,3},{6,4},{4,6},{7,5},{5,7},{10,8},{8,10},{11,... | collective-permute-start | bytes 6152 | tf_op jit(solution)/shard_map/while/body/eval_jaxpr/ppermute | solution.py:30
  99.1 4.4 %collective-permute-start = (bf16[1,256,128]{1,2,0:T(8,128)(2,1)S(1)}, bf16[1,256,128]{1,2,0:T(8,128)(2,1)S(1)}, u32[]{:S(2)}, u32[]{:S(2)}) collective-permute-start(bf16[1,256,128]{1,2,0:T(8,128)(2,1)S(1)} %fusion.66), channel_id=1, source_target_pairs={{1,0},{3,2},{5,4},{7,6},{9,8},{11,10},{13,12},{15,14},{17,16},{19,... | collective-permute-start | bytes 196616 | tf_op jit(solution)/shard_map/while/body/eval_jaxpr/ppermute | solution.py:17
  100.4 3.9 %collective-permute-start.1 = (bf16[1,256,128]{1,2,0:T(8,128)(2,1)S(1)}, bf16[1,256,128]{1,2,0:T(8,128)(2,1)S(1)}, u32[]{:S(2)}, u32[]{:S(2)}) collective-permute-start(bf16[1,256,128]{1,2,0:T(8,128)(2,1)S(1)} %fusion.66), channel_id=1, source_target_pairs={{0,1},{2,3},{4,5},{6,7},{8,9},{10,11},{12,13},{14,15},{16,17},{18,... | collective-permute-start | bytes 196616 | tf_op jit(solution)/shard_map/while/body/eval_jaxpr/ppermute | solution.py:16
  104.4 5.7 %collective-permute-start.2 = (bf16[1,256,128]{1,2,0:T(8,128)(2,1)S(1)}, bf16[1,256,128]{1,2,0:T(8,128)(2,1)S(1)}, u32[]{:S(2)}, u32[]{:S(2)}) collective-permute-start(bf16[1,256,128]{1,2,0:T(8,128)(2,1)S(1)} %get-tuple-element.591), channel_id=1, source_target_pairs={{2,0},{0,2},{3,1},{1,3},{6,4},{4,6},{7,5},{5,7},{10,8},{8,10},{11,... | collective-permute-start | bytes 196616 | tf_op jit(solution)/shard_map/while/body/eval_jaxpr/ppermute | solution.py:30
  106.2 3.8 %collective-permute-start.3 = (bf16[1,77,128]{2,1,0:T(8,128)(2,1)S(1)}, bf16[1,77,128]{2,1,0:T(8,128)(2,1)S(1)}, u32[]{:S(2)}, u32[]{:S(2)}) collective-permute-start(bf16[1,77,128]{2,1,0:T(8,128)(2,1)S(1)} %fusion.65), channel_id=1, source_target_pairs={{2,0},{0,2},{3,1},{1,3},{6,4},{4,6},{7,5},{5,7},{10,8},{8,10},{11,... | collective-permute-start | bytes 59144 | tf_op jit(solution)/shard_map/while/body/eval_jaxpr/ppermute | solution.py:30
  106.5 3.6 %collective-permute-start.4 = (bf16[2,1,4,128]{3,2,1,0:T(4,128)(2,1)S(1)}, bf16[2,1,4,128]{3,2,1,0:T(4,128)(2,1)S(1)}, u32[]{:S(2)}, u32[]{:S(2)}) collective-permute-start(bf16[2,1,4,128]{3,2,1,0:T(4,128)(2,1)S(1)} %copy.34), channel_id=1, source_target_pairs={{2,0},{0,2},{3,1},{1,3},{6,4},{4,6},{7,5},{5,7},{10,8},{8,10},{11,... | collective-permute-start | bytes 6152 | tf_op jit(solution)/shard_map/while/body/eval_jaxpr/ppermute | solution.py:30
where the time goes:
time: 129 us; the launch traced here: 128 us
  starting transfers between devices  43.7 us (34%)
  blocking collectives  29.7 us (23%)
  waiting for transfers between devices  22.4 us (17%)
  matrix products  17 us (13%)
  local copies, waits for them, and re-layouts  7.54 us (6%)
  other arithmetic  3.66 us (3%)
  between operations  2.62 us (2%)
    ppermute x6, starting transfers between devices, padded_2(): before = lax.ppermute(last, axis, up)  18.2 us
    ppermute x18, starting transfers between devices, passed_along(): return lax.ppermute(block, axis, route)  17.7 us
    ppermute x18, waiting for transfers between devices, passed_along(): return lax.ppermute(block, axis, route)  17.2 us
    psum x1, blocking collectives, per_device(): lax.psum(ocean_state.astype(jnp.float32).astype(jnp.bfloat16), 'members')  16.2 us
    psum x1, blocking collectives, from_root(): return lax.psum(jnp.where(mine, array, jnp.zeros_like(array)), axis)  13.5 us
    ppermute x6, starting transfers between devices, padded_2(): after = lax.ppermute(initial, axis, down)  7.75 us
    dot_general x6, matrix products, encode(): jnp.einsum('ok,lkx->lox', encode_weight, inputs, preferred_element_type=j...  5.99 us
    dot_general x6, matrix products, decode(): jnp.einsum('ok,lkx->lox', decode_weight, hidden, preferred_element_type=j...  5.64 us
  transfers between devices with their start and end apart: 30, of which 12 were waited for; matrix products, arithmetic and copies ran while one was open for 0% of the time, Pallas kernels for 0%

commit v1 on v0

v1 whole, which is shorter than its diff:
```python
import functools

import jax
import jax.numpy as jnp
from jax import lax
from jax.experimental import pallas as pl
from jax.experimental.pallas import tpu as pltpu
from jax.sharding import PartitionSpec as P

STEPS = 2
CONV_CHUNKS = 4
MESH = pl.DeviceIdType.MESH


def to_column(row):
    size = row.shape[1]
    at = lax.broadcasted_iota(jnp.int32, (size, size), 0)
    along = lax.broadcasted_iota(jnp.int32, (size, size), 1)
    return jnp.sum(jnp.where(at == along, row, 0.0), axis=1, keepdims=True)


def shifted(field, offset):
    if offset == 0:
        return field
    lon = field.shape[1]
    place = lax.broadcasted_iota(jnp.int32, field.shape, 1)
    moved = pltpu.roll(field, (-offset) % lon, 1)
    return jnp.where((place + offset >= 0) & (place + offset < lon), moved, 0.0)


def kernel(
    sizes,
    init_ref,
    slots_ref,
    owner_ref,
    land_ref,
    param_ref,
    settings_ref,
    scale_ref,
    shift_ref,
    encode_ref,
    conv_ref,
    point_ref,
    gain_ref,
    decode_ref,
    final_ref,
    mean_ref,
    conv_all,
    point_all,
    gain_all,
    init_other,
    land_other,
    force_all,
    final_all,
    inputs,
    taps,
    pair_send,
    pair_recv,
    force_send,
    force_recv,
    seg_send,
    seg_recv,
    grp_send,
    grp_recv,
    core_send,
    core_recv,
    gain_send,
    gain_recv,
    mean_send,
    mean_recv,
    own_sem,
):
    groups, members, segments, rows = sizes
    g = lax.axis_index("groups")
    m = lax.axis_index("members")
    s = lax.axis_index("segment")
    r = lax.axis_index("rows")
    channels = conv_all.shape[1]
    lon = init_ref.shape[3]

    def ahead(value, step, size):
        return lax.rem(value + step, size)

    def device(dg=0, dm=0, ds=0, dr=0):
        return (
            ahead(g, dg, groups),
            ahead(m, dm, members),
            ahead(s, ds, segments),
            ahead(r, dr, rows),
        )

    mates = [(dm, dr) for dm in range(members) for dr in range(rows) if dm or dr]
    barrier = pltpu.get_barrier_semaphore()
    met = 0
    for dm, dr in mates:
        pl.semaphore_signal(barrier, inc=1, device_id=device(dm=dm, dr=dr), device_id_type=MESH)
        met += 1
    for ds in range(1, segments):
        pl.semaphore_signal(barrier, inc=1, device_id=device(ds=ds), device_id_type=MESH)
        met += 1
    for dg in range(1, groups):
        pl.semaphore_signal(barrier, inc=1, device_id=device(dg=dg), device_id_type=MESH)
        met += 1
    pl.semaphore_wait(barrier, met)

    def send(source, target, send_sem, recv_sem, to):
        return pltpu.make_async_remote_copy(
            src_ref=source,
            dst_ref=target,
            send_sem=send_sem,
            recv_sem=recv_sem,
            device_id=to,
            device_id_type=MESH,
        )

    share = channels // (groups * rows)
    chunk = share // CONV_CHUNKS

    def piece(group, row, index):
        start = (group * rows + row) * share
        if index < CONV_CHUNKS:
            return pl.ds(pl.multiple_of(start + index * chunk, chunk), chunk)
        return pl.ds(pl.multiple_of(start, share), share)

    def view(layer, group, row, index):
        part = conv_all if index < CONV_CHUNKS else point_all
        return part.at[layer, piece(group, row, index)]

    def source_view(index):
        part = conv_ref if index < CONV_CHUNKS else point_ref
        return part.at[0, piece(g, r, index)]

    pieces = range(CONV_CHUNKS + 1)
    seg_copies = {}
    for index in pieces:
        for ds in range(1, segments):
            copy = send(
                source_view(index),
                view(s, g, r, index),
                seg_send.at[ds - 1, index],
                seg_recv.at[ds - 1, index],
                device(ds=ds),
            )
            copy.start()
            seg_copies[ds, index] = copy
    others = []
    other_row = device(dr=1)
    init_copy = send(init_ref.at[0, 0], init_other, pair_send.at[0], pair_recv.at[0], other_row)
    land_copy = send(land_ref, land_other, pair_send.at[1], pair_recv.at[1], other_row)
    others += [init_copy, land_copy]
    for index, (dm, dr) in enumerate(mates):
        others.append(
            send(
                slots_ref.at[0, 0, :, 0],
                force_all.at[m, r],
                force_send.at[index],
                force_recv.at[index],
                device(dm=dm, dr=dr),
            )
        )
    for ds in range(1, segments):
        others.append(
            send(gain_ref, gain_all.at[s], gain_send.at[ds - 1], gain_recv.at[ds - 1], device(ds=ds))
        )
    for copy in others:
        copy.start()
    own = [
        pltpu.make_async_copy(conv_ref.at[0], conv_all.at[s], own_sem.at[0]),
        pltpu.make_async_copy(point_ref.at[0], point_all.at[s], own_sem.at[1]),
        pltpu.make_async_copy(gain_ref, gain_all.at[s], own_sem.at[2]),
        pltpu.make_async_copy(slots_ref.at[0, 0, :, 0], force_all.at[m, r], own_sem.at[3]),
    ]
    for copy in own:
        copy.start()

    chosen = lax.broadcasted_iota(jnp.int32, settings_ref.shape, 0) == param_ref[0]
    setting_row = jnp.sum(jnp.where(chosen, settings_ref[...], 0.0), axis=0, keepdims=True)
    setting = to_column(setting_row)
    cond_scale = to_column(1.0 + jnp.sum(setting * scale_ref[...], axis=0, keepdims=True))
    cond_shift = to_column(jnp.sum(setting * shift_ref[...], axis=0, keepdims=True))
    encode_weight = encode_ref[...]
    decode_weight = decode_ref[...]
    for copy in others:
        copy.wait()
    for copy in own:
        copy.wait()

    head = r == 0
    mine, theirs = init_ref[0, 0].astype(jnp.float32), init_other[...].astype(jnp.float32)
    state = jnp.concatenate(
        [jnp.where(head, mine, theirs), jnp.where(head, theirs, mine)], axis=1
    )
    land_mine = land_ref[...].astype(jnp.float32)
    land_theirs = land_other[...].astype(jnp.float32)
    land = jnp.concatenate(
        [jnp.where(head, land_mine, land_theirs), jnp.where(head, land_theirs, land_mine)], axis=1
    )
    variables = state.shape[0]
    forces = slots_ref.shape[4]

    def encoded(state, step_no):
        owner = owner_ref[0, step_no]
        inputs[0:variables, :] = state
        for row in range(rows):
            total = jnp.zeros((forces, lon), jnp.float32)
            for member in range(members):
                slot = force_all[member, row, step_no].astype(jnp.float32)
                total = total + jnp.where(owner == member, slot, 0.0)
            inputs[variables : variables + forces, row * lon : (row + 1) * lon] = total
        fields = inputs[...][: variables + forces].astype(jnp.bfloat16)
        lifted = jnp.dot(encode_weight, fields, preferred_element_type=jnp.float32)
        return (land * (lifted * cond_scale + cond_shift)).astype(jnp.bfloat16)

    hidden = encoded(state, 0)

    relays = []
    for index in pieces:
        for ds in range(1, segments):
            layer = lax.rem(s - ds + segments, segments)
            seg_copies[ds, index].wait_recv()
            here = view(layer, g, r, index)
            grp = {}
            for dg in range(1, groups):
                copy = send(
                    here,
                    here,
                    grp_send.at[ds - 1, dg - 1, index],
                    grp_recv.at[ds - 1, dg - 1, index],
                    device(dg=dg),
                )
                copy.start()
                grp[dg] = copy
            copy = send(
                here,
                here,
                core_send.at[ds - 1, 0, index],
                core_recv.at[ds - 1, 0, index],
                other_row,
            )
            copy.start()
            relays.append((layer, ds, index, grp, copy))
    waits = []
    for layer, ds, index, grp, copy in relays:
        waits.append(copy)
        for dg in range(1, groups):
            grp[dg].wait_recv()
            there = view(layer, lax.rem(g - dg + groups, groups), r, index)
            relay = send(
                there,
                there,
                core_send.at[ds - 1, dg, index],
                core_recv.at[ds - 1, dg, index],
                other_row,
            )
            relay.start()
            waits.append(relay)
    for copy in waits:
        copy.wait_recv()

    for step_no in range(STEPS):
        if step_no:
            hidden = encoded(state, step_no)
        for layer in range(segments):
            spacing = 2 ** (layer % 3)
            wide = hidden.astype(jnp.float32)
            for row in range(rows):
                here = wide[:, row * lon : (row + 1) * lon]
                for at, offset in enumerate((-spacing, 0, spacing)):
                    taps[at * channels : (at + 1) * channels, row * lon : (row + 1) * lon] = shifted(
                        here, offset
                    ).astype(jnp.bfloat16)
            span = 3 * channels
            conv = jnp.dot(
                conv_all[layer, :, span : 2 * span], taps[...], preferred_element_type=jnp.float32
            )
            below = jnp.dot(
                conv_all[layer, :, 2 * span :], taps[:, lon:], preferred_element_type=jnp.float32
            )
            above = jnp.dot(
                conv_all[layer, :, :span], taps[:, :lon], preferred_element_type=jnp.float32
            )
            conv = conv + jnp.concatenate([below, above], axis=1)
            centred = conv - jnp.mean(conv, axis=0, keepdims=True)
            spread = jnp.mean(centred * centred, axis=0, keepdims=True)
            gain = to_column(gain_all[layer].astype(jnp.float32))
            normed = centred * lax.rsqrt(spread + 1e-05) * gain
            activated = jax.nn.gelu(normed).astype(jnp.bfloat16)
            mixed = jnp.dot(point_all[layer], activated, preferred_element_type=jnp.float32)
            hidden = (land * (wide + mixed)).astype(jnp.bfloat16)
        change = jnp.dot(decode_weight, hidden, preferred_element_type=jnp.float32)
        state = (state + land * change).astype(jnp.bfloat16).astype(jnp.float32)

    own_final = jnp.where(head, state[:, :lon], state[:, lon:])
    final_ref[0, 0, 0] = own_final.astype(jnp.bfloat16)
    mean_copies = []
    for dm in range(1, members):
        copy = send(
            final_ref.at[0, 0, 0],
            final_all.at[m],
            mean_send.at[dm - 1],
            mean_recv.at[dm - 1],
            device(dm=dm),
        )
        copy.start()
        mean_copies.append(copy)
    final_all[m] = own_final.astype(jnp.bfloat16)
    for copy in seg_copies.values():
        copy.wait_send()
    for layer, ds, index, grp, copy in relays:
        for dg in range(1, groups):
            grp[dg].wait_send()
    for copy in waits:
        copy.wait_send()
    for copy in mean_copies:
        copy.wait()
    total = jnp.zeros(own_final.shape, jnp.float32)
    for member in range(members):
        total = total + final_all[member].astype(jnp.float32)
    mean_ref[0, 0] = total / members


def solution(mesh):
    sizes = tuple(mesh.shape[axis] for axis in ("groups", "members", "segment", "rows"))
    groups, members, segments, rows = sizes

    def per_device(*args):
        init, slots, conv = args[0], args[1], args[9]
        variables, lon = init.shape[2:]
        forces = slots.shape[4]
        channels = conv.shape[1]
        vmem = pl.BlockSpec(memory_space=pltpu.VMEM)
        smem = pl.BlockSpec(memory_space=pltpu.SMEM)
        hbm = pl.BlockSpec(memory_space=pl.ANY)
        in_specs = [vmem] * 13
        in_specs[2] = in_specs[4] = smem
        in_specs[9] = in_specs[10] = hbm
        dma = pltpu.SemaphoreType.DMA
        pieces = CONV_CHUNKS + 1
        mates = members * rows - 1
        away = max(segments - 1, 1)
        scratch = [
            pltpu.VMEM((segments,) + conv.shape[1:], jnp.bfloat16),
            pltpu.VMEM((segments, channels, channels), jnp.bfloat16),
            pltpu.VMEM((segments, 1, channels), jnp.bfloat16),
            pltpu.VMEM((variables, lon), jnp.bfloat16),
            pltpu.VMEM((1, lon), jnp.int32),
            pltpu.VMEM((members, rows, STEPS, forces, lon), jnp.bfloat16),
            pltpu.VMEM((members, variables, lon), jnp.bfloat16),
            pltpu.VMEM((-(-(variables + forces) // 8) * 8, rows * lon), jnp.float32),
            pltpu.VMEM((3 * channels, rows * lon), jnp.bfloat16),
            dma((2,)),
            dma((2,)),
            dma((mates,)),
            dma((mates,)),
            dma((away, pieces)),
            dma((away, pieces)),
            dma((away, max(groups - 1, 1), pieces)),
            dma((away, max(groups - 1, 1), pieces)),
            dma((away, groups, pieces)),
            dma((away, groups, pieces)),
            dma((away,)),
            dma((away,)),
            dma((max(members - 1, 1),)),
            dma((max(members - 1, 1),)),
            dma((4,)),
        ]
        return pl.pallas_call(
            functools.partial(kernel, sizes),
            out_shape=(
                jax.ShapeDtypeStruct((1, 1, 1, variables, lon), jnp.bfloat16),
                jax.ShapeDtypeStruct((1, 1, variables, lon), jnp.float32),
            ),
            in_specs=in_specs,
            out_specs=(vmem, vmem),
            scratch_shapes=scratch,
            compiler_params=pltpu.CompilerParams(
                collective_id=0, has_side_effects=True, vmem_limit_bytes=48 * 1024 * 1024
            ),
        )(*args)

    in_specs = (
        P(("groups", "segment"), "rows", None, None),
        P("members", ("groups", "segment"), None, "rows", None, None),
        P(("groups", "segment"), None),
        P(("groups", "rows"), None),
        P(("groups", "members")),
        P(),
        P(),
        P(),
        P(),
        P("segment", None, None),
        P("segment", None, None),
        P("segment", None),
        P(),
    )
    out_specs = (
        P("members", ("groups", "segment"), "rows", None, None),
        P(("groups", "segment"), "rows", None, None),
    )
    return jax.shard_map(
        per_device, mesh=mesh, in_specs=in_specs, out_specs=out_specs, check_vma=False
    )
```

time: 129 us -> 44.8 us (0.35)
  starting transfers between devices: 43.7 us -> 0 us
  Pallas kernels: 0 us -> 32.2 us
  blocking collectives: 29.7 us -> 0 us
  waiting for transfers between devices: 22.4 us -> 0 us
  matrix products: 17 us -> 0 us
  other arithmetic: 3.66 us -> 0 us
  local copies, waits for them, and re-layouts: 7.54 us -> 10.7 us
  between operations: 2.62 us -> 1.3 us
    ppermute x30 -> x0, starting transfers between devices: 43.7 us -> none  [the longest x6 18.2 us: padded_2(): before = lax.ppermute(last, axis, up)]
    pallas_call x0 -> x1, Pallas kernels: none -> 32.2 us  [per_device(): pl.pallas_call(functools.partial(kernel, sizes), out_shape=(jax.ShapeDtyp...]
    psum x2 -> x0, blocking collectives: 29.7 us -> none  [the longest x1 16.2 us: per_device(): lax.psum(ocean_state.astype(jnp.float32).astype(jnp.bfloat16), 'members')]
    ppermute x30 -> x0, waiting for transfers between devices: 22.4 us -> none  [the longest x18 17.2 us: passed_along(): return lax.ppermute(block, axis, route)]
    dot_general x23 -> x0, matrix products: 17 us -> none  [the longest x6 5.99 us: encode(): jnp.einsum('ok,lkx->lox', encode_weight, inputs, preferred_element_type=j...]
    unnamed x4 -> x23, local copies, waits for them, and re-layouts: 1.35 us -> 10.1 us
    cond x48 -> x0, local copies, waits for them, and re-layouts: 2.91 us -> none
    slice x5 -> x0, local copies, waits for them, and re-layouts: 2.08 us -> none  [the longest x1 1.31 us: per_device(): atmos_owner[0, step_no]]
  transfers between devices with their start and end apart: 30 -> 0, of which waited for: 12 -> 0; matrix products, arithmetic and copies ran while one was open for 0% -> 0% of each run, Pallas kernels for 0% -> 0%
where the time goes in v1:
time: 44.8 us; the launch traced here: 44.2 us
  Pallas kernels  32.2 us (72%)
  local copies, waits for them, and re-layouts  10.7 us (24%)
  between operations  1.3 us (3%)
    pallas_call x1, Pallas kernels, per_device(): pl.pallas_call(functools.partial(kernel, sizes), out_shape=(jax.ShapeDtyp...  32.2 us
    unnamed x23, local copies, waits for them, and re-layouts  10.1 us

profile of v1, /device:TPU:0, one launch (start us, length us, event | category | flops | bytes accessed | tf_op | source)
XLA Modules:
  0.0 44.2 jit_solution(7993917050580930519)
XLA Ops:
  1.3 0.8 %copy.15.settings_ref = f32[64,16]{1,0:T(8,128)S(1)} copy(f32[64,16]{0,1:T(8,128)} %param.18) | data formatting | bytes 8192 | tf_op args[5]
  2.1 0.9 %copy.16.encode_ref = bf16[256,81]{1,0:T(8,128)(2,1)S(1)} copy(bf16[256,81]{0,1:T(8,128)(2,1)} %param.21) | data formatting | bytes 82944 | tf_op args[8]
  3.0 0.0 copy-start
  3.0 1.3 %copy-done = bf16[1,256,2304]{2,1,0:T(8,128)(2,1)S(1)} copy-done((bf16[1,256,2304]{2,1,0:T(8,128)(2,1)S(1)}, bf16[1,256,2304]{2,1,0:T(8,128)(2,1)}, u32[]{:S(2)}) %copy-start) | copy-done | bytes 1179672
  4.2 0.0 copy-start.1
  4.3 0.9 %copy-done.1 = bf16[1,256,256]{2,1,0:T(8,128)(2,1)S(1)} copy-done((bf16[1,256,256]{2,1,0:T(8,128)(2,1)S(1)}, bf16[1,256,256]{2,1,0:T(8,128)(2,1)}, u32[]{:S(2)}) %copy-start.1) | copy-done | bytes 131096
  5.2 0.0 copy-start.2
  5.2 0.8 %copy-done.2 = bf16[77,256]{1,0:T(8,128)(2,1)S(1)} copy-done((bf16[77,256]{1,0:T(8,128)(2,1)S(1)}, bf16[77,256]{1,0:T(8,128)(2,1)}, u32[]{:S(2)}) %copy-start.2) | copy-done | bytes 39448
  5.9 0.0 copy-start.3
  5.9 0.7 %copy-done.3 = bf16[1,1,77,128]{3,2,1,0:T(8,128)(2,1)S(1)} copy-done((bf16[1,1,77,128]{3,2,1,0:T(8,128)(2,1)S(1)}, bf16[1,1,77,128]{3,2,1,0:T(8,128)(2,1)}, u32[]{:S(2)}) %copy-start.3) | copy-done | bytes 19736
  6.7 0.0 copy-start.4
  6.7 0.7 %copy-done.4 = f32[16,256]{1,0:T(8,128)S(1)} copy-done((f32[16,256]{1,0:T(8,128)S(1)}, f32[16,256]{1,0:T(8,128)}, u32[]{:S(2)}) %copy-start.4) | copy-done | bytes 16408
  7.4 0.0 copy-start.5
  7.4 0.7 %copy-done.5 = f32[16,256]{1,0:T(8,128)S(1)} copy-done((f32[16,256]{1,0:T(8,128)S(1)}, f32[16,256]{1,0:T(8,128)}, u32[]{:S(2)}) %copy-start.5) | copy-done | bytes 16408
  8.1 0.0 copy-start.6
  8.1 0.7 %copy-done.6 = bf16[1,1,2,1,4,128]{5,4,3,2,1,0:T(4,128)(2,1)S(1)} copy-done((bf16[1,1,2,1,4,128]{5,4,3,2,1,0:T(4,128)(2,1)S(1)}, bf16[1,1,2,1,4,128]{5,4,3,2,1,0:T(4,128)(2,1)}, u32[]{:S(2)}) %copy-start.6) | copy-done | bytes 2072
  8.8 0.0 copy-start.7
  8.8 0.7 %copy-done.7 = bf16[1,256]{1,0:T(2,128)(2,1)S(1)} copy-done((bf16[1,256]{1,0:T(2,128)(2,1)S(1)}, bf16[1,256]{1,0:T(2,128)(2,1)}, u32[]{:S(2)}) %copy-start.7) | copy-done | bytes 536
  9.5 0.0 copy-start.8
  9.5 0.7 %copy-done.8 = s32[1,2]{1,0:T(1,128)S(1)} copy-done((s32[1,2]{1,0:T(1,128)S(1)}, s32[1,2]{1,0:T(1,128)}, u32[]{:S(2)}) %copy-start.8) | copy-done | bytes 32
  10.1 0.0 copy-start.9
  10.1 0.7 %copy-done.9 = s32[1,128]{1,0:T(1,128)S(1)} copy-done((s32[1,128]{1,0:T(1,128)S(1)}, s32[1,128]{1,0:T(1,128)}, u32[]{:S(2)}) %copy-start.9) | copy-done | bytes 536
  10.8 32.2 %shard_map.140 = (bf16[1,1,1,77,128]{4,3,2,1,0:T(8,128)(2,1)S(1)}, f32[1,1,77,128]{3,2,1,0:T(8,128)S(1)}) custom-call(bf16[1,1,77,128]{3,2,1,0:T(8,128)(2,1)S(1)} %copy-done.3, bf16[1,1,2,1,4,128]{5,4,3,2,1,0:T(4,128)(2,1)S(1)} %copy-done.6, s32[1,2]{1,0:T(1,128)S(1)} %copy-done.8, s32[1,128]{1,0:T(1,128)S(1)} %copy-done.9, s32[1]{0:T(128)S(6)} %copy.19.param_ref, ...), custom_call_target="tpu_custom_call" | custom-call | tf_op jit(solution)/shard_map/pallas_call | solution.py:367
  42.9 0.7 %copy.17 = f32[1,1,77,128]{3,1,2,0:T(1,128)} copy(f32[1,1,77,128]{3,2,1,0:T(8,128)S(1)} %get-tuple-element.3) | data formatting | bytes 78848 | tf_op jit(solution)/shard_map/pallas_call | solution.py:367
  43.6 0.6 %copy.20 = bf16[1,1,1,77,128]{4,3,2,1,0:T(8,128)(2,1)} copy(bf16[1,1,1,77,128]{4,3,2,1,0:T(8,128)(2,1)S(1)} %get-tuple-element.6) | data formatting | bytes 39424
Async XLA Ops:
  3.0 1.3 %copy-start = (bf16[1,256,2304]{2,1,0:T(8,128)(2,1)S(1)}, bf16[1,256,2304]{2,1,0:T(8,128)(2,1)}, u32[]{:S(2)}) copy-start(bf16[1,256,2304]{2,1,0:T(8,128)(2,1)} %conv_ref.1) | copy-start | bytes 3538948
  4.2 0.9 %copy-start.1 = (bf16[1,256,256]{2,1,0:T(8,128)(2,1)S(1)}, bf16[1,256,256]{2,1,0:T(8,128)(2,1)}, u32[]{:S(2)}) copy-start(bf16[1,256,256]{2,1,0:T(8,128)(2,1)} %point_ref.1) | copy-start | bytes 393220
  5.2 0.8 %copy-start.2 = (bf16[77,256]{1,0:T(8,128)(2,1)S(1)}, bf16[77,256]{1,0:T(8,128)(2,1)}, u32[]{:S(2)}) copy-start(bf16[77,256]{1,0:T(8,128)(2,1)} %decode_ref.1) | copy-start | bytes 118276
  5.9 0.7 %copy-start.3 = (bf16[1,1,77,128]{3,2,1,0:T(8,128)(2,1)S(1)}, bf16[1,1,77,128]{3,2,1,0:T(8,128)(2,1)}, u32[]{:S(2)}) copy-start(bf16[1,1,77,128]{3,2,1,0:T(8,128)(2,1)} %init_ref.1) | copy-start | bytes 59140
  6.7 0.7 %copy-start.4 = (f32[16,256]{1,0:T(8,128)S(1)}, f32[16,256]{1,0:T(8,128)}, u32[]{:S(2)}) copy-start(f32[16,256]{1,0:T(8,128)} %scale_ref.1) | copy-start | bytes 49156
  7.4 0.7 %copy-start.5 = (f32[16,256]{1,0:T(8,128)S(1)}, f32[16,256]{1,0:T(8,128)}, u32[]{:S(2)}) copy-start(f32[16,256]{1,0:T(8,128)} %shift_ref.1) | copy-start | bytes 49156
  8.1 0.7 %copy-start.6 = (bf16[1,1,2,1,4,128]{5,4,3,2,1,0:T(4,128)(2,1)S(1)}, bf16[1,1,2,1,4,128]{5,4,3,2,1,0:T(4,128)(2,1)}, u32[]{:S(2)}) copy-start(bf16[1,1,2,1,4,128]{5,4,3,2,1,0:T(4,128)(2,1)} %slots_ref.1) | copy-start | bytes 6148
  8.8 0.7 %copy-start.7 = (bf16[1,256]{1,0:T(2,128)(2,1)S(1)}, bf16[1,256]{1,0:T(2,128)(2,1)}, u32[]{:S(2)}) copy-start(bf16[1,256]{1,0:T(2,128)(2,1)} %gain_ref.1) | copy-start | bytes 1540
  9.5 0.7 %copy-start.8 = (s32[1,2]{1,0:T(1,128)S(1)}, s32[1,2]{1,0:T(1,128)}, u32[]{:S(2)}) copy-start(s32[1,2]{1,0:T(1,128)} %owner_ref.1) | copy-start | bytes 28
  10.1 0.7 %copy-start.9 = (s32[1,128]{1,0:T(1,128)S(1)}, s32[1,128]{1,0:T(1,128)}, u32[]{:S(2)}) copy-start(s32[1,128]{1,0:T(1,128)} %land_ref.1) | copy-start | bytes 1540

commit v2 on v1

--- a/solution.py
+++ b/solution.py
@@ -30,8 +30,22 @@
 
 def kernel(
     sizes,
+    init_hbm,
+    slots_ref,
+    owner_hbm,
+    land_hbm,
+    param_hbm,
+    settings_hbm,
+    scale_hbm,
+    shift_hbm,
+    encode_hbm,
+    conv_ref,
+    point_ref,
+    gain_ref,
+    decode_hbm,
+    final_ref,
+    mean_ref,
     init_ref,
-    slots_ref,
     owner_ref,
     land_ref,
     param_ref,
@@ -39,12 +53,7 @@
     scale_ref,
     shift_ref,
     encode_ref,
-    conv_ref,
-    point_ref,
-    gain_ref,
     decode_ref,
-    final_ref,
-    mean_ref,
     conv_all,
     point_all,
     gain_all,
@@ -76,7 +85,7 @@
     s = lax.axis_index("segment")
     r = lax.axis_index("rows")
     channels = conv_all.shape[1]
-    lon = init_ref.shape[3]
+    lon = init_hbm.shape[3]
 
     def ahead(value, step, size):
         return lax.rem(value + step, size)
@@ -88,6 +97,27 @@
             ahead(s, ds, segments),
             ahead(r, dr, rows),
         )
+
+    fetched = [
+        (owner_hbm, owner_ref),
+        (param_hbm, param_ref),
+        (settings_hbm, settings_ref),
+        (scale_hbm, scale_ref),
+        (shift_hbm, shift_ref),
+        (encode_hbm, encode_ref),
+        (init_hbm, init_ref),
+        (land_hbm, land_ref),
+        (decode_hbm, decode_ref),
+        (gain_ref, gain_all.at[s]),
+        (slots_ref.at[0, 0, :, 0], force_all.at[m, r]),
+        (conv_ref.at[0], conv_all.at[s]),
+        (point_ref.at[0], point_all.at[s]),
+    ]
+    own = []
+    for index, (source, target) in enumerate(fetched):
+        copy = pltpu.make_async_copy(source, target, own_sem.at[index])
+        copy.start()
+        own.append(copy)
 
     mates = [(dm, dr) for dm in range(members) for dr in range(rows) if dm or dr]
     barrier = pltpu.get_barrier_semaphore()
@@ -145,8 +175,8 @@
             seg_copies[ds, index] = copy
     others = []
     other_row = device(dr=1)
-    init_copy = send(init_ref.at[0, 0], init_other, pair_send.at[0], pair_recv.at[0], other_row)
-    land_copy = send(land_ref, land_other, pair_send.at[1], pair_recv.at[1], other_row)
+    init_copy = send(init_hbm.at[0, 0], init_other, pair_send.at[0], pair_recv.at[0], other_row)
+    land_copy = send(land_hbm, land_other, pair_send.at[1], pair_recv.at[1], other_row)
     others += [init_copy, land_copy]
     for index, (dm, dr) in enumerate(mates):
         others.append(
@@ -164,25 +194,15 @@
         )
     for copy in others:
         copy.start()
-    own = [
-        pltpu.make_async_copy(conv_ref.at[0], conv_all.at[s], own_sem.at[0]),
-        pltpu.make_async_copy(point_ref.at[0], point_all.at[s], own_sem.at[1]),
-        pltpu.make_async_copy(gain_ref, gain_all.at[s], own_sem.at[2]),
-        pltpu.make_async_copy(slots_ref.at[0, 0, :, 0], force_all.at[m, r], own_sem.at[3]),
-    ]
     for copy in own:
-        copy.start()
-
-    chosen = lax.broadcasted_iota(jnp.int32, settings_ref.shape, 0) == param_ref[0]
-    setting_row = jnp.sum(jnp.where(chosen, settings_ref[...], 0.0), axis=0, keepdims=True)
-    setting = to_column(setting_row)
+        copy.wait()
+    chosen = lax.broadcasted_iota(jnp.int32, settings_ref.shape, 1) == param_ref[0]
+    setting = jnp.sum(jnp.where(chosen, settings_ref[...], 0.0), axis=1, keepdims=True)
     cond_scale = to_column(1.0 + jnp.sum(setting * scale_ref[...], axis=0, keepdims=True))
     cond_shift = to_column(jnp.sum(setting * shift_ref[...], axis=0, keepdims=True))
     encode_weight = encode_ref[...]
     decode_weight = decode_ref[...]
     for copy in others:
-        copy.wait()
-    for copy in own:
         copy.wait()
 
     head = r == 0
@@ -208,7 +228,9 @@
                 total = total + jnp.where(owner == member, slot, 0.0)
             inputs[variables : variables + forces, row * lon : (row + 1) * lon] = total
         fields = inputs[...][: variables + forces].astype(jnp.bfloat16)
-        lifted = jnp.dot(encode_weight, fields, preferred_element_type=jnp.float32)
+        lifted = lax.dot_general(
+            encode_weight, fields, (((0,), (0,)), ((), ())), preferred_element_type=jnp.float32
+        )
         return (land * (lifted * cond_scale + cond_shift)).astype(jnp.bfloat16)
 
     hidden = encoded(state, 0)
@@ -329,16 +351,19 @@
         forces = slots.shape[4]
         channels = conv.shape[1]
         vmem = pl.BlockSpec(memory_space=pltpu.VMEM)
-        smem = pl.BlockSpec(memory_space=pltpu.SMEM)
-        hbm = pl.BlockSpec(memory_space=pl.ANY)
-        in_specs = [vmem] * 13
-        in_specs[2] = in_specs[4] = smem
-        in_specs[9] = in_specs[10] = hbm
+        hbm = pl.BlockSpec(memory_space=pltpu.HBM)
+        args = list(args)
+        args[5] = args[5].T
+        args[8] = args[8].T
         dma = pltpu.SemaphoreType.DMA
         pieces = CONV_CHUNKS + 1
         mates = members * rows - 1
         away = max(segments - 1, 1)
-        scratch = [
+        local = [
+            pltpu.SMEM(args[i].shape, args[i].dtype) if i in (2, 4) else pltpu.VMEM(args[i].shape, args[i].dtype)
+            for i in (0, 2, 3, 4, 5, 6, 7, 8, 12)
+        ]
+        scratch = local + [
             pltpu.VMEM((segments,) + conv.shape[1:], jnp.bfloat16),
             pltpu.VMEM((segments, channels, channels), jnp.bfloat16),
             pltpu.VMEM((segments, 1, channels), jnp.bfloat16),
@@ -362,7 +387,7 @@
             dma((away,)),
             dma((max(members - 1, 1),)),
             dma((max(members - 1, 1),)),
-            dma((4,)),
+            dma((13,)),
         ]
         return pl.pallas_call(
             functools.partial(kernel, sizes),
@@ -370,11 +395,11 @@
                 jax.ShapeDtypeStruct((1, 1, 1, variables, lon), jnp.bfloat16),
                 jax.ShapeDtypeStruct((1, 1, variables, lon), jnp.float32),
             ),
-            in_specs=in_specs,
+            in_specs=[hbm] * 13,
             out_specs=(vmem, vmem),
             scratch_shapes=scratch,
             compiler_params=pltpu.CompilerParams(
-                collective_id=0, has_side_effects=True, vmem_limit_bytes=48 * 1024 * 1024
+                collective_id=0, has_side_effects=True
             ),
         )(*args)
 

time: 44.8 us -> 36.9 us (0.82)
  local copies, waits for them, and re-layouts: 10.7 us -> 2.77 us
    unnamed x23 -> x1, local copies, waits for them, and re-layouts: 10.1 us -> 1.33 us
    pallas_call x1, local copies, waits for them, and re-layouts: 0.66 us -> 1.44 us  [per_device(): pl.pallas_call(functools.partial(kernel, sizes), out_shape=(jax.ShapeDtyp...]
where the time goes in v2:
time: 36.9 us; the launch traced here: 36.6 us
  Pallas kernels  32.6 us (88%)
  local copies, waits for them, and re-layouts  2.77 us (8%)
  between operations  1.29 us (3%)
    pallas_call x1, Pallas kernels, per_device(): pl.pallas_call(functools.partial(kernel, sizes), out_shape=(jax.ShapeDtyp...  32.6 us
    pallas_call x1, local copies, waits for them, and re-layouts, per_device(): pl.pallas_call(functools.partial(kernel, sizes), out_shape=(jax.ShapeDtyp...  1.44 us
    unnamed x1, local copies, waits for them, and re-layouts  1.33 us

profile of v2, /device:TPU:0, one launch (start us, length us, event | category | flops | bytes accessed | tf_op | source)
XLA Modules:
  0.0 36.6 jit_solution(7764706410739470386)
XLA Ops:
  1.3 32.6 %shard_map.140 = (bf16[1,1,1,77,128]{4,3,2,1,0:T(8,128)(2,1)}, f32[1,1,77,128]{3,2,1,0:T(8,128)}) custom-call(bf16[1,1,77,128]{3,2,1,0:T(8,128)(2,1)} %init_hbm.1, bf16[1,1,2,1,4,128]{5,4,3,2,1,0:T(4,128)(2,1)} %slots_ref.1, s32[1,2]{1,0:T(1,128)} %owner_hbm.1, s32[1,128]{1,0:T(1,128)} %land_hbm.1, s32[1]{0:T(128)S(6)} %copy.17.param_hbm, f32[16,64]{1,0:T(8,128)} %bitcast.3, ...), custom_call_target="tpu_custom_call" | custom-call | tf_op jit(solution)/shard_map/pallas_call | solution.py:392
  33.9 1.4 %copy.15 = f32[1,1,77,128]{3,1,2,0:T(1,128)} copy(f32[1,1,77,128]{3,2,1,0:T(8,128)} %get-tuple-element.3) | data formatting | bytes 78848 | tf_op jit(solution)/shard_map/pallas_call | solution.py:392
  35.3 1.3 %copy.18 = bf16[1,1,1,77,128]{4,3,2,1,0:T(8,128)(2,1)} copy(bf16[1,1,1,77,128]{4,3,2,1,0:T(8,128)(2,1)} %get-tuple-element.6) | data formatting | bytes 39424
